TPU v7x, 32 devices: a whole 2x2x4 slice. The times are simulated.
32 devices in a mesh: row: 4 (over y, x), col: 8 (over z, core).
Axes of the slice: x: 2, y: 2, z: 4, core: 2. Of those that a mesh axis runs over, the one named last changes fastest.
Arguments:
- event_bins: bfloat16 [2048, 64], P(('row', 'col')), may hold values from -15 to 15
- counts: int32 [2048], P(('row', 'col')), may hold values from 1 to 8
- hidden_weight: bfloat16 [64, 1024], replicated, may hold values from -0.75 to 0.75
- hidden_bias: float32 [1024], replicated, may hold values from -4 to 4
- feature_weight: bfloat16 [1024, 256], replicated, may hold values from -0.1875 to 0.1875
Outputs:
- factor: float32 [2048, 2048], P('row', 'col')
All inputs are finite; a program needn't handle non-finite values.
Results may differ from a plain program's by a relative error of at most 0.0037.
Values may be sent and summed in bfloat16 or wider, within the bound.
A program may use at most 64 MiB of HBM per device.

v0:
```python
import jax
import jax.numpy as jnp
from jax import lax
from jax.experimental import pallas as pl
from jax.experimental.pallas import tpu as pltpu
from jax.sharding import PartitionSpec as P

kernel_offset = 0.25
root_five = 5.0**0.5
BLK = 128
SLAB = 16
SUB = 8
F32 = jnp.float32
BF16 = jnp.bfloat16


def split(x):
    hi = x.astype(BF16)
    return hi, (x - hi.astype(F32)).astype(BF16)


def dot_nt(a, b):
    return lax.dot_general(a, b, (((1,), (1,)), ((), ())), preferred_element_type=F32)


def dot3(a, b):
    return dot_nt(a[0], b[0]) + (dot_nt(a[0], b[1]) + dot_nt(a[1], b[0]))


def factor_block(work, upper, fillers):
    lanes = (SUB, BLK)
    sub = lax.broadcasted_iota(jnp.int32, (SUB, 2 * BLK), 0)
    slabs = BLK // SLAB
    for s in range(slabs):
        base = s * SLAB
        slab = work[base : base + SLAB, :]
        sq = {}
        for j in range(SLAB):
            lane = base + j
            column = jnp.broadcast_to(slab[:, lane : lane + 1], (SLAB, BLK))
            for i in range(j, SLAB):
                sq[i, j] = jnp.broadcast_to(column[i : i + 1, :], lanes)
        low, inv = {}, []
        rows = [jnp.broadcast_to(slab[i : i + 1, :], (SUB, 2 * BLK)) for i in range(SLAB)]
        parts = [None] * (SLAB // SUB)
        for j in range(SLAB):
            inv.append(lax.rsqrt(sq[j, j]))
            for i in range(j + 1, SLAB):
                low[i, j] = sq[i, j] * inv[j]
            for i in range(j + 1, SLAB):
                for m in range(j + 1, i + 1):
                    sq[i, m] = sq[i, m] - low[i, j] * low[m, j]
            rows[j] = rows[j] * jnp.concatenate([inv[j], inv[j]], axis=1)
            for i in range(j + 1, SLAB):
                rows[i] = rows[i] - jnp.concatenate([low[i, j], low[i, j]], axis=1) * rows[j]
            g = j // SUB
            parts[g] = rows[j] if j % SUB == 0 else jnp.where(sub == j % SUB, rows[j], parts[g])
        done = jnp.concatenate(parts, axis=0) if len(parts) > 1 else parts[0]
        upper[base : base + SLAB, :] = done
        nxt = base + SLAB
        if nxt < BLK:
            hi = done.astype(BF16).astype(F32)
            lo = done - hi
            odd = SLAB % 16 != 0
            pad_left = [jnp.zeros((SLAB, BLK), F32)] if odd else []
            pad_right = [jnp.zeros((SLAB, 2 * BLK), F32)] if odd else []
            left = jnp.concatenate([hi[:, :BLK], hi[:, :BLK], lo[:, :BLK]] + pad_left, axis=0)
            right = jnp.concatenate([hi, lo, hi] + pad_right, axis=0)
            change = lax.dot_general(
                left.astype(BF16), right.astype(BF16), (((0,), (0,)), ((), ())), preferred_element_type=F32
            )
        for filler in fillers[s * len(fillers) // slabs : (s + 1) * len(fillers) // slabs]:
            filler()
        if nxt < BLK:
            work[nxt:, :] = work[nxt:, :] - change[nxt:, :]


def main_kernel(
    pw, d_in, bins, w1, bias, w2, out, f_hi, f_lo, sq_col, sq_row, sc_col, sc_row, stack, cur, work, upper,
    x_hi, x_lo, inv_hi, inv_lo,
):
    tile = 2 * pw
    row_index, col_index = lax.axis_index("row"), lax.axis_index("col")
    row_start, col_start = row_index * tile, col_index * pw
    feat = w2.shape[1]
    chunks = (2 * tile + pw) // BLK
    lead_chunks = tile // BLK
    starts = [t * BLK for t in range(lead_chunks)]
    starts += [row_start + t * BLK for t in range(lead_chunks)]
    starts += [col_start + t * BLK for t in range(pw // BLK)]
    ones = jnp.ones((SUB, feat), BF16)
    pick = (lax.broadcasted_iota(jnp.int32, (SUB, bins.shape[1] - d_in), 1) == 0).astype(F32).astype(BF16)

    def embed(t):
        start = starts[t]
        at = pl.ds(start if isinstance(start, int) else pl.multiple_of(start, BLK), BLK)
        here = slice(t * BLK, (t + 1) * BLK)
        pre = jnp.dot(bins[at, 0:d_in], w1[...], preferred_element_type=F32) + bias[...]
        hidden = jax.nn.gelu(pre).astype(BF16)
        f = jnp.dot(hidden, w2[...], preferred_element_type=F32)
        f_hi[here, :], f_lo[here, :] = split(f)
        ff = f * f
        sq_col[here, :] = jnp.sum(ff, axis=1, keepdims=True)
        p1 = ff.astype(BF16)
        p2, p3 = split(ff - p1.astype(F32))
        sq_row[:, here] = dot_nt(ones, p1) + (dot_nt(ones, p2) + dot_nt(ones, p3))
        cnt = bins[at, d_in:]
        sc_col[here, :] = jnp.sqrt(cnt[:, 0:1].astype(F32))
        sc_row[:, here] = jnp.sqrt(dot_nt(pick, cnt))

    def window(a0, n, b0, m, left_id, right_id):
        la, rb = pl.ds(a0, n), pl.ds(b0, m)
        inner = dot3((f_hi[la, :], f_lo[la, :]), (f_hi[rb, :], f_lo[rb, :]))
        dist = jnp.maximum(sq_col[la, :] + sq_row[0:1, rb] - 2.0 * inner, 0.0)
        q = dist * (4.0 / feat)
        r = jnp.sqrt(q)
        matern = (1.0 + root_five * r + 5.0 / 3.0 * q) * jnp.exp(-root_five * r)
        ids = left_id + lax.broadcasted_iota(jnp.int32, (n, m), 0)
        jds = right_id + lax.broadcasted_iota(jnp.int32, (n, m), 1)
        return (ids == jds).astype(F32) + sc_col[la, :] * sc_row[0:1, rb] * (matern + kernel_offset)

    def lead_window(t):
        stack[t * BLK : (t + 1) * BLK, :] = window(t * BLK, BLK, 0, tile, starts[t], 0)

    def cur_window(h):
        cur[h * BLK : (h + 1) * BLK, :] = window(
            tile + h * BLK, BLK, 2 * tile, pw, row_start + h * BLK, col_start
        )

    def pair(rows, cols):
        return x_hi[rows, cols], x_lo[rows, cols]

    def place(b):
        return pl.ds(b * BLK if isinstance(b, int) else pl.multiple_of(b * BLK, BLK), BLK)

    def solve(rows, b):
        panel = dot3(split(stack[rows, place(b)]), (inv_hi[...], inv_lo[...]))
        x_hi[rows, place(b)], x_lo[rows, place(b)] = split(panel)

    def reduce(rows, b):
        stack[rows, place(b)] = stack[rows, place(b)] - dot3(
            pair(rows, slice(None)), pair(place(b), slice(None))
        )

    def downdate(h, b):
        rows = slice(tile + h * BLK, tile + (h + 1) * BLK)
        here = slice(h * BLK, (h + 1) * BLK)
        cur[here, :] = cur[here, :] - dot3(pair(rows, place(b)), pair(slice(2 * tile, None), place(b)))

    def finish(b):
        inv_hi[...], inv_lo[...] = split(upper[:, BLK:])
        solve(slice(0, tile), b)

    work[:, BLK:] = (
        lax.broadcasted_iota(jnp.int32, (BLK, BLK), 0) == lax.broadcasted_iota(jnp.int32, (BLK, BLK), 1)
    ).astype(F32)
    for t in range(lead_chunks):
        embed(t)
    for t in range(lead_chunks):
        lead_window(t)
    x_hi[...] = jnp.zeros_like(x_hi)
    x_lo[...] = jnp.zeros_like(x_lo)

    outer = range(lead_chunks, chunks)
    fillers = [lambda t=t: embed(t) for t in outer] + [lambda t=t: lead_window(t) for t in outer]
    fillers += [lambda h=h: cur_window(h) for h in range(lead_chunks)]
    work[:, :BLK] = stack[0:BLK, 0:BLK]
    factor_block(work, upper, fillers)
    finish(0)

    def step(b, carry):
        work[:, :BLK] = stack[place(b), place(b)] - dot3(
            pair(place(b), slice(None)), pair(place(b), slice(None))
        )
        work[:, BLK:] = (
            lax.broadcasted_iota(jnp.int32, (BLK, BLK), 0) == lax.broadcasted_iota(jnp.int32, (BLK, BLK), 1)
        ).astype(F32)

        def advance(t):
            rows = slice(t * BLK, (t + 1) * BLK)
            solve(rows, b - 1)
            reduce(rows, b)

        tasks = [lambda t=t: reduce(slice(t * BLK, (t + 1) * BLK), b) for t in range(lead_chunks)]
        tasks += [lambda t=t: advance(t) for t in outer]
        tasks += [lambda h=h: downdate(h, b - 1) for h in range(lead_chunks)]
        factor_block(work, upper, tasks)
        finish(b)
        return carry

    lax.fori_loop(1, lead_chunks, step, 0)

    is_lead = row_index == 0
    last = lead_chunks - 1

    def write_panel(c):
        cols = slice(c * pw, (c + 1) * pw)

        @pl.when((col_index == c) & is_lead)
        def _():
            ids = lax.broadcasted_iota(jnp.int32, (tile, pw), 0)
            jds = lax.broadcasted_iota(jnp.int32, (tile, pw), 1) + c * pw
            whole = x_hi[0:tile, cols].astype(F32) + x_lo[0:tile, cols].astype(F32)
            out[...] = jnp.where(ids >= jds, whole, 0.0)

        @pl.when((col_index == c) & jnp.logical_not(is_lead))
        def _():
            solve(slice(tile, 2 * tile), last)
            out[...] = x_hi[tile : 2 * tile, cols].astype(F32) + x_lo[tile : 2 * tile, cols].astype(F32)

    write_panel(0)
    write_panel(1)

    @pl.when((col_index >= 2) & is_lead)
    def _():
        out[...] = jnp.zeros((tile, pw), F32)

    @pl.when((col_index >= 2) & jnp.logical_not(is_lead))
    def _():
        solve(slice(tile, None), last)
        out[...] = cur[...] - dot3(
            pair(slice(tile, 2 * tile), place(last)), pair(slice(2 * tile, None), place(last))
        )


def gather_kernel(x_ref, o_ref, own_sem, send_sem, pass_sem, recv_sem):
    rows, cols = lax.axis_size("row"), lax.axis_size("col")
    my_row, my_col = lax.axis_index("row"), lax.axis_index("col")
    me = my_row * cols + my_col
    total = rows * cols
    height = x_ref.shape[0]

    def block(g):
        return o_ref.at[pl.ds(pl.multiple_of(g * height, height), height), :]

    def direct(source, row, col):
        same_row = source // cols == row
        lead = (source // cols == 0) & (source % cols == col)
        return same_row | lead | ((source // cols != 0) & (source // rows == col))

    def needs(source, row, col):
        return direct(source, row, col) | (source // cols == 0)

    def send_copy(target):
        return pltpu.make_async_remote_copy(
            src_ref=x_ref,
            dst_ref=block(me),
            send_sem=send_sem.at[target],
            recv_sem=recv_sem.at[me],
            device_id=(target // cols, target % cols),
            device_id_type=pl.DeviceIdType.MESH,
        )

    barrier = pltpu.get_barrier_semaphore()
    own = pltpu.make_async_copy(x_ref, block(me), own_sem)
    own.start()

    def greet(d, c):
        other = (me + d) % total
        pl.semaphore_signal(
            barrier, inc=1, device_id=(other // cols, other % cols), device_id_type=pl.DeviceIdType.MESH
        )
        return c

    lax.fori_loop(1, total, greet, 0)
    pl.semaphore_wait(barrier, total - 1)

    def send(d, c):
        target = (me + d) % total

        @pl.when(direct(me, target // cols, target % cols))
        def _():
            send_copy(target).start()

        return c

    lax.fori_loop(1, total, send, 0)

    def pass_copy(d):
        to_col = (my_col + d) % cols
        return pltpu.make_async_remote_copy(
            src_ref=block(my_col),
            dst_ref=block(my_col),
            send_sem=pass_sem.at[to_col],
            recv_sem=recv_sem.at[my_col],
            device_id=(my_row, to_col),
            device_id_type=pl.DeviceIdType.MESH,
        )

    @pl.when(my_row != 0)
    def _():
        pltpu.make_async_remote_copy(
            src_ref=x_ref,
            dst_ref=block(my_col),
            send_sem=send_sem.at[my_col],
            recv_sem=recv_sem.at[my_col],
            device_id=(0, my_col),
            device_id_type=pl.DeviceIdType.MESH,
        ).wait_recv()

        def forward(d, c):
            pass_copy(d).start()
            return c

        lax.fori_loop(1, cols, forward, 0)

    own.wait()

    def receive(d, c):
        source = (me + total - d) % total

        @pl.when(needs(source, my_row, my_col) & ((my_row == 0) | (source != my_col)))
        def _():
            pltpu.make_async_remote_copy(
                src_ref=x_ref,
                dst_ref=block(source),
                send_sem=send_sem.at[source],
                recv_sem=recv_sem.at[source],
                device_id=(source // cols, source % cols),
                device_id_type=pl.DeviceIdType.MESH,
            ).wait_recv()

        return c

    lax.fori_loop(1, total, receive, 0)

    def drain(d, c):
        target = (me + d) % total

        @pl.when(direct(me, target // cols, target % cols))
        def _():
            send_copy(target).wait_send()

        return c

    lax.fori_loop(1, total, drain, 0)

    @pl.when(my_row != 0)
    def _():
        def drain_pass(d, c):
            pass_copy(d).wait_send()
            return c

        lax.fori_loop(1, cols, drain_pass, 0)


def gather_bins(packed):
    total = lax.axis_size("row") * lax.axis_size("col")
    anywhere = pl.BlockSpec(memory_space=pl.ANY)
    return pl.pallas_call(
        gather_kernel,
        out_shape=jax.ShapeDtypeStruct((packed.shape[0] * total, packed.shape[1]), packed.dtype),
        in_specs=[anywhere],
        out_specs=anywhere,
        scratch_shapes=[
            pltpu.SemaphoreType.DMA,
            pltpu.SemaphoreType.DMA((total,)),
            pltpu.SemaphoreType.DMA((lax.axis_size("col"),)),
            pltpu.SemaphoreType.DMA((total,)),
        ],
        compiler_params=pltpu.CompilerParams(collective_id=0, has_side_effects=True),
    )(packed)


def per_device(event_bins, counts, hidden_weight, hidden_bias, feature_weight):
    d_in = event_bins.shape[1]
    col_count, row_count = lax.axis_size("col"), lax.axis_size("row")
    tile = event_bins.shape[0] * col_count
    pw = tile * row_count // col_count
    feat = feature_weight.shape[1]
    wide = jnp.broadcast_to(counts.astype(BF16)[:, None], (counts.shape[0], 128 - d_in))
    packed = jnp.concatenate([event_bins, wide], axis=1)
    bins = gather_bins(packed)
    n = 2 * tile + pw
    vm = pl.BlockSpec(memory_space=pltpu.VMEM)
    return pl.pallas_call(
        lambda *refs: main_kernel(pw, d_in, *refs),
        out_shape=jax.ShapeDtypeStruct((tile, pw), F32),
        in_specs=[vm] * 4,
        out_specs=vm,
        scratch_shapes=[
            pltpu.VMEM((n, feat), BF16),
            pltpu.VMEM((n, feat), BF16),
            pltpu.VMEM((n, 1), F32),
            pltpu.VMEM((SUB, n), F32),
            pltpu.VMEM((n, 1), F32),
            pltpu.VMEM((SUB, n), F32),
            pltpu.VMEM((n, tile), F32),
            pltpu.VMEM((tile, pw), F32),
            pltpu.VMEM((BLK, 2 * BLK), F32),
            pltpu.VMEM((BLK, 2 * BLK), F32),
            pltpu.VMEM((n, tile), BF16),
            pltpu.VMEM((n, tile), BF16),
            pltpu.VMEM((BLK, BLK), BF16),
            pltpu.VMEM((BLK, BLK), BF16),
        ],
        compiler_params=pltpu.CompilerParams(vmem_limit_bytes=60 * 1024 * 1024),
    )(bins, hidden_weight, hidden_bias.reshape(1, -1), feature_weight)


def solution(mesh):
    in_specs = (P(("row", "col"), None), P(("row", "col")), P(), P(), P())
    return jax.shard_map(
        per_device, mesh=mesh, in_specs=in_specs, out_specs=P("row", "col"), check_vma=False
    )
```

profile of v0, /device:TPU:11, one launch (start us, length us, event | category | flops | bytes accessed | tf_op | source)
XLA Modules:
  0.0 50.8 jit_solution(4535060657331862220)
XLA Ops:
  0.0 0.0 copy-start.1
  0.0 0.0 copy-start
  0.0 0.7 %copy-done.1 = s32[64]{0:T(128)S(1)} copy-done((s32[64]{0:T(128)S(1)}, s32[64]{0:T(128)}, u32[]{:S(2)}) %copy-start.1) | copy-done | bytes 280
  0.7 0.1 broadcast_in_dim.2
  0.7 0.0 copy-done
  0.7 0.7 %pad_maximum_fusion.x_ref = bf16[64,128]{1,0:T(8,128)(2,1)} fusion(bf16[64,64]{1,0:T(8,128)(2,1)S(1)} %broadcast_in_dim.2, bf16[64,64]{1,0:T(8,128)(2,1)S(1)} %copy-done), kind=kLoop, calls=%fused_computation | loop fusion | flops 32768 | bytes 32768 | tf_op jit(solution)/shard_map/concatenate | solution.py:372
  1.4 14.7 %shard_map.55.refs_0_ = bf16[2048,128]{1,0:T(8,128)(2,1)} custom-call(bf16[64,128]{1,0:T(8,128)(2,1)} %pad_maximum_fusion.x_ref), custom_call_target="tpu_custom_call" | custom-call | tf_op jit(solution)/shard_map/pallas_call | solution.py:350
  16.1 34.7 %shard_map.56 = f32[512,256]{1,0:T(8,128)} custom-call(bf16[2048,128]{1,0:T(8,128)(2,1)} %shard_map.55.refs_0_, bf16[64,1024]{1,0:T(8,128)(2,1)} %refs_1_.1, f32[1,1024]{1,0:T(1,128)} %bitcast.1, bf16[1024,256]{1,0:T(8,128)(2,1)} %refs_3_.1), custom_call_target="tpu_custom_call" | custom-call | tf_op jit(solution)/shard_map/pallas_call | solution.py:376
  (1 shorter events, 0.0 us)
Async XLA Ops:
  0.0 0.7 %copy-start.1 = (s32[64]{0:T(128)S(1)}, s32[64]{0:T(128)}, u32[]{:S(2)}) copy-start(s32[64]{0:T(128)} %param.6) | copy-start | bytes 772
  0.0 0.7 %copy-start = (bf16[64,64]{1,0:T(8,128)(2,1)S(1)}, bf16[64,64]{1,0:T(8,128)(2,1)}, u32[]{:S(2)}) copy-start(bf16[64,64]{1,0:T(8,128)(2,1)} %param.5) | copy-start | bytes 24580
where the time goes:
time: 51 us; the launch traced here: 50.8 us
  Pallas kernels  49.3 us (97%)
  local copies, waits for them, and re-layouts  0.73 us (1%)
  other arithmetic  0.69 us (1%)
    pallas_call x1, Pallas kernels, per_device(): pl.pallas_call(lambda *refs: main_kernel(pw, d_in, *refs), out_shape=jax....  34.7 us
    pallas_call x1, Pallas kernels, gather_bins(): pl.pallas_call(gather_kernel, out_shape=jax.ShapeDtypeStruct((packed.shap...  14.7 us

commit v1 on v0

--- a/solution.py
+++ b/solution.py
@@ -8,7 +8,7 @@
 kernel_offset = 0.25
 root_five = 5.0**0.5
 BLK = 128
-SLAB = 16
+SUP = 32
 SUB = 8
 F32 = jnp.float32
 BF16 = jnp.bfloat16
@@ -27,49 +27,68 @@
     return dot_nt(a[0], b[0]) + (dot_nt(a[0], b[1]) + dot_nt(a[1], b[0]))
 
 
+def spread(x, j):
+    return jnp.broadcast_to(x[j : j + 1, :], x.shape)
+
+def eliminate(left, right, base):
+    groups = len(left)
+    left, right = list(left), list(right)
+    sub = lax.broadcasted_iota(jnp.int32, (SUB, BLK), 0)
+    out = []
+    for k in range(groups):
+        col = {}
+        for t in range(k, groups):
+            for m in range(SUB):
+                lane = base + k * SUB + m
+                col[t, m] = jnp.broadcast_to(left[t][:, lane : lane + 1], (SUB, BLK))
+        keep = [None, None]
+        for j in range(0, SUB, 2):
+            a, b = col[k, j], col[k, j + 1]
+            p, q, r = spread(a, j), spread(a, j + 1), spread(b, j + 1)
+            det = p * r - q * q
+            ip, ih = lax.rsqrt(p), lax.rsqrt(det)
+            ip_ih = ip * ih
+            alpha, beta = r * a - q * b, p * b - q * a
+            ih2 = ih * ih
+            la, lb = {k: a * ip}, {k: beta * ip_ih}
+            for t in range(k + 1, groups):
+                la[t] = col[t, j] * ip
+                lb[t] = (p * col[t, j + 1] - q * col[t, j]) * ip_ih
+            for m in range(j + 2, SUB):
+                both = alpha * spread(a, m) + beta * spread(b, m)
+                col[k, m] = col[k, m] - both * ih2
+                if k + 1 < groups:
+                    sa, sb = spread(la[k], m), spread(lb[k], m)
+                    for t in range(k + 1, groups):
+                        col[t, m] = col[t, m] - (la[t] * sa + lb[t] * sb)
+            for h, side in enumerate((left, right)):
+                first, second = spread(side[k], j), spread(side[k], j + 1)
+                ua = first * ip
+                ub = (p * second - q * first) * ip_ih
+                keep[h] = ua if j == 0 else jnp.where(sub == j, ua, keep[h])
+                keep[h] = jnp.where(sub == j + 1, ub, keep[h])
+                for t in range(k if j + 2 < SUB else k + 1, groups):
+                    side[t] = side[t] - (la[t] * ua + lb[t] * ub)
+        out.append(keep)
+    return jnp.concatenate([o[0] for o in out], axis=0), jnp.concatenate([o[1] for o in out], axis=0)
+
 def factor_block(work, upper, fillers):
-    lanes = (SUB, BLK)
-    sub = lax.broadcasted_iota(jnp.int32, (SUB, 2 * BLK), 0)
-    slabs = BLK // SLAB
-    for s in range(slabs):
-        base = s * SLAB
-        slab = work[base : base + SLAB, :]
-        sq = {}
-        for j in range(SLAB):
-            lane = base + j
-            column = jnp.broadcast_to(slab[:, lane : lane + 1], (SLAB, BLK))
-            for i in range(j, SLAB):
-                sq[i, j] = jnp.broadcast_to(column[i : i + 1, :], lanes)
-        low, inv = {}, []
-        rows = [jnp.broadcast_to(slab[i : i + 1, :], (SUB, 2 * BLK)) for i in range(SLAB)]
-        parts = [None] * (SLAB // SUB)
-        for j in range(SLAB):
-            inv.append(lax.rsqrt(sq[j, j]))
-            for i in range(j + 1, SLAB):
-                low[i, j] = sq[i, j] * inv[j]
-            for i in range(j + 1, SLAB):
-                for m in range(j + 1, i + 1):
-                    sq[i, m] = sq[i, m] - low[i, j] * low[m, j]
-            rows[j] = rows[j] * jnp.concatenate([inv[j], inv[j]], axis=1)
-            for i in range(j + 1, SLAB):
-                rows[i] = rows[i] - jnp.concatenate([low[i, j], low[i, j]], axis=1) * rows[j]
-            g = j // SUB
-            parts[g] = rows[j] if j % SUB == 0 else jnp.where(sub == j % SUB, rows[j], parts[g])
-        done = jnp.concatenate(parts, axis=0) if len(parts) > 1 else parts[0]
-        upper[base : base + SLAB, :] = done
-        nxt = base + SLAB
+    sups = BLK // SUP
+    for s in range(sups):
+        base = s * SUP
+        rows = [slice(base + t * SUB, base + (t + 1) * SUB) for t in range(SUP // SUB)]
+        ua, ui = eliminate([work[r, :BLK] for r in rows], [work[r, BLK:] for r in rows], base)
+        upper[base : base + SUP, :BLK] = ua
+        upper[base : base + SUP, BLK:] = ui
+        nxt = base + SUP
         if nxt < BLK:
-            hi = done.astype(BF16).astype(F32)
-            lo = done - hi
-            odd = SLAB % 16 != 0
-            pad_left = [jnp.zeros((SLAB, BLK), F32)] if odd else []
-            pad_right = [jnp.zeros((SLAB, 2 * BLK), F32)] if odd else []
-            left = jnp.concatenate([hi[:, :BLK], hi[:, :BLK], lo[:, :BLK]] + pad_left, axis=0)
-            right = jnp.concatenate([hi, lo, hi] + pad_right, axis=0)
-            change = lax.dot_general(
-                left.astype(BF16), right.astype(BF16), (((0,), (0,)), ((), ())), preferred_element_type=F32
-            )
-        for filler in fillers[s * len(fillers) // slabs : (s + 1) * len(fillers) // slabs]:
+            done = jnp.concatenate([ua, ui], axis=1)
+            hi = done.astype(BF16)
+            lo = (done - hi.astype(F32)).astype(BF16)
+            left = jnp.concatenate([hi[:, :BLK], hi[:, :BLK], lo[:, :BLK]], axis=0)
+            right = jnp.concatenate([hi, lo, hi], axis=0)
+            change = lax.dot_general(left, right, (((0,), (0,)), ((), ())), preferred_element_type=F32)
+        for filler in fillers[s * len(fillers) // sups : (s + 1) * len(fillers) // sups]:
             filler()
         if nxt < BLK:
             work[nxt:, :] = work[nxt:, :] - change[nxt:, :]

time: 51 us -> 47.4 us (0.929)
  Pallas kernels: 49.3 us -> 45.7 us
    pallas_call x1, Pallas kernels: 34.7 us -> 31 us  [per_device(): pl.pallas_call(lambda *refs: main_kernel(pw, d_in, *refs), out_shape=jax....]
where the time goes in v1:
time: 47.4 us; the launch traced here: 47.1 us
  Pallas kernels  45.7 us (96%)
  local copies, waits for them, and re-layouts  0.73 us (2%)
  other arithmetic  0.69 us (1%)
    pallas_call x1, Pallas kernels, per_device(): pl.pallas_call(lambda *refs: main_kernel(pw, d_in, *refs), out_shape=jax....  31 us
    pallas_call x1, Pallas kernels, gather_bins(): pl.pallas_call(gather_kernel, out_shape=jax.ShapeDtypeStruct((packed.shap...  14.7 us

profile of v1, /device:TPU:11, one launch (start us, length us, event | category | flops | bytes accessed | tf_op | source)
XLA Modules:
  0.0 47.1 jit_solution(18200218382194412719)
XLA Ops:
  0.0 0.0 copy-start.1
  0.0 0.0 copy-start
  0.0 0.7 %copy-done.1 = s32[64]{0:T(128)S(1)} copy-done((s32[64]{0:T(128)S(1)}, s32[64]{0:T(128)}, u32[]{:S(2)}) %copy-start.1) | copy-done | bytes 280
  0.7 0.1 broadcast_in_dim.2
  0.7 0.0 copy-done
  0.7 0.7 %pad_maximum_fusion.x_ref = bf16[64,128]{1,0:T(8,128)(2,1)} fusion(bf16[64,64]{1,0:T(8,128)(2,1)S(1)} %broadcast_in_dim.2, bf16[64,64]{1,0:T(8,128)(2,1)S(1)} %copy-done), kind=kLoop, calls=%fused_computation | loop fusion | flops 32768 | bytes 32768 | tf_op jit(solution)/shard_map/concatenate | solution.py:391
  1.4 14.7 %shard_map.55.refs_0_ = bf16[2048,128]{1,0:T(8,128)(2,1)} custom-call(bf16[64,128]{1,0:T(8,128)(2,1)} %pad_maximum_fusion.x_ref), custom_call_target="tpu_custom_call" | custom-call | tf_op jit(solution)/shard_map/pallas_call | solution.py:369
  16.1 31.0 %shard_map.56 = f32[512,256]{1,0:T(8,128)} custom-call(bf16[2048,128]{1,0:T(8,128)(2,1)} %shard_map.55.refs_0_, bf16[64,1024]{1,0:T(8,128)(2,1)} %refs_1_.1, f32[1,1024]{1,0:T(1,128)} %bitcast.1, bf16[1024,256]{1,0:T(8,128)(2,1)} %refs_3_.1), custom_call_target="tpu_custom_call" | custom-call | tf_op jit(solution)/shard_map/pallas_call | solution.py:395
  (1 shorter events, 0.0 us)
Async XLA Ops:
  0.0 0.7 %copy-start.1 = (s32[64]{0:T(128)S(1)}, s32[64]{0:T(128)}, u32[]{:S(2)}) copy-start(s32[64]{0:T(128)} %param.6) | copy-start | bytes 772
  0.0 0.7 %copy-start = (bf16[64,64]{1,0:T(8,128)(2,1)S(1)}, bf16[64,64]{1,0:T(8,128)(2,1)}, u32[]{:S(2)}) copy-start(bf16[64,64]{1,0:T(8,128)(2,1)} %param.5) | copy-start | bytes 24580

commit v2 on v1

--- a/solution.py
+++ b/solution.py
@@ -1,3 +1,5 @@
+import math
+
 import jax
 import jax.numpy as jnp
 from jax import lax
@@ -6,7 +8,10 @@
 from jax.sharding import PartitionSpec as P
 
 kernel_offset = 0.25
-root_five = 5.0**0.5
+gelu_linear = (2.0 / math.pi) ** 0.5
+gelu_cubic = 0.044715 * gelu_linear
+log2_e = math.log2(math.e)
+tiny = 1e-30
 BLK = 128
 SUP = 32
 SUB = 8
@@ -30,7 +35,7 @@
 def spread(x, j):
     return jnp.broadcast_to(x[j : j + 1, :], x.shape)
 
-def eliminate(left, right, base):
+def eliminate(left, right, base, zero):
     groups = len(left)
     left, right = list(left), list(right)
     sub = lax.broadcasted_iota(jnp.int32, (SUB, BLK), 0)
@@ -41,6 +46,8 @@
             for m in range(SUB):
                 lane = base + k * SUB + m
                 col[t, m] = jnp.broadcast_to(left[t][:, lane : lane + 1], (SUB, BLK))
+                if t == k and m < 2:
+                    col[t, m] = col[t, m] + zero
         keep = [None, None]
         for j in range(0, SUB, 2):
             a, b = col[k, j], col[k, j + 1]
@@ -72,12 +79,13 @@
         out.append(keep)
     return jnp.concatenate([o[0] for o in out], axis=0), jnp.concatenate([o[1] for o in out], axis=0)
 
-def factor_block(work, upper, fillers):
+def factor_block(work, upper, zeros, fillers):
+    zero = zeros[...]
     sups = BLK // SUP
     for s in range(sups):
         base = s * SUP
         rows = [slice(base + t * SUB, base + (t + 1) * SUB) for t in range(SUP // SUB)]
-        ua, ui = eliminate([work[r, :BLK] for r in rows], [work[r, BLK:] for r in rows], base)
+        ua, ui = eliminate([work[r, :BLK] for r in rows], [work[r, BLK:] for r in rows], base, zero)
         upper[base : base + SUP, :BLK] = ua
         upper[base : base + SUP, BLK:] = ui
         nxt = base + SUP
@@ -95,13 +103,14 @@
 
 
 def main_kernel(
-    pw, d_in, bins, w1, bias, w2, out, f_hi, f_lo, sq_col, sq_row, sc_col, sc_row, stack, cur, work, upper,
-    x_hi, x_lo, inv_hi, inv_lo,
+    pw, d_in, bins, w1, bias, w2, out, feats, sq_col, sq_row, sc_col, sc_row, stack, cur, work, upper,
+    x_hi, x_lo, inv_hi, inv_lo, zeros,
 ):
     tile = 2 * pw
     row_index, col_index = lax.axis_index("row"), lax.axis_index("col")
     row_start, col_start = row_index * tile, col_index * pw
     feat = w2.shape[1]
+    reach = (5.0 / feat) ** 0.5
     chunks = (2 * tile + pw) // BLK
     lead_chunks = tile // BLK
     starts = [t * BLK for t in range(lead_chunks)]
@@ -115,42 +124,47 @@
         at = pl.ds(start if isinstance(start, int) else pl.multiple_of(start, BLK), BLK)
         here = slice(t * BLK, (t + 1) * BLK)
         pre = jnp.dot(bins[at, 0:d_in], w1[...], preferred_element_type=F32) + bias[...]
-        hidden = jax.nn.gelu(pre).astype(BF16)
-        f = jnp.dot(hidden, w2[...], preferred_element_type=F32)
-        f_hi[here, :], f_lo[here, :] = split(f)
-        ff = f * f
+        inner = pre * (gelu_linear + gelu_cubic * (pre * pre))
+        hidden = (pre * (1.0 + jnp.tanh(inner))).astype(BF16)
+        f = (jnp.dot(hidden, w2[...], preferred_element_type=F32) * reach).astype(BF16)
+        feats[here, :] = f
+        wide = f.astype(F32)
+        ff = wide * wide
         sq_col[here, :] = jnp.sum(ff, axis=1, keepdims=True)
-        p1 = ff.astype(BF16)
-        p2, p3 = split(ff - p1.astype(F32))
-        sq_row[:, here] = dot_nt(ones, p1) + (dot_nt(ones, p2) + dot_nt(ones, p3))
+        p1, p2 = split(ff)
+        sq_row[:, here] = dot_nt(ones, p1) + dot_nt(ones, p2)
         cnt = bins[at, d_in:]
         sc_col[here, :] = jnp.sqrt(cnt[:, 0:1].astype(F32))
         sc_row[:, here] = jnp.sqrt(dot_nt(pick, cnt))
 
-    def window(a0, n, b0, m, left_id, right_id):
-        la, rb = pl.ds(a0, n), pl.ds(b0, m)
-        inner = dot3((f_hi[la, :], f_lo[la, :]), (f_hi[rb, :], f_lo[rb, :]))
-        dist = jnp.maximum(sq_col[la, :] + sq_row[0:1, rb] - 2.0 * inner, 0.0)
-        q = dist * (4.0 / feat)
-        r = jnp.sqrt(q)
-        matern = (1.0 + root_five * r + 5.0 / 3.0 * q) * jnp.exp(-root_five * r)
-        ids = left_id + lax.broadcasted_iota(jnp.int32, (n, m), 0)
-        jds = right_id + lax.broadcasted_iota(jnp.int32, (n, m), 1)
-        return (ids == jds).astype(F32) + sc_col[la, :] * sc_row[0:1, rb] * (matern + kernel_offset)
+    def window(a0, n, b0, m):
+        la, rb = slice(a0, a0 + n), slice(b0, b0 + m)
+        inner = dot_nt(feats[la, :] * (-2.0), feats[rb, :])
+        t2 = jnp.maximum(sq_col[la, :] + sq_row[0:1, rb] + inner, tiny)
+        t = t2 * lax.rsqrt(t2)
+        matern = (1.0 + t + t2 * (1.0 / 3.0)) * jnp.exp2(t * (-log2_e))
+        return sc_col[la, :] * sc_row[0:1, rb] * (matern + kernel_offset)
+
+    def diagonal(n, m, shift):
+        ids = shift + lax.broadcasted_iota(jnp.int32, (n, m), 0)
+        return (ids == lax.broadcasted_iota(jnp.int32, (n, m), 1)).astype(F32)
 
     def lead_window(t):
-        stack[t * BLK : (t + 1) * BLK, :] = window(t * BLK, BLK, 0, tile, starts[t], 0)
+        part = window(t * BLK, BLK, 0, tile)
+        if t < lead_chunks:
+            part = part + diagonal(BLK, tile, t * BLK)
+        stack[t * BLK : (t + 1) * BLK, :] = part
 
     def cur_window(h):
-        cur[h * BLK : (h + 1) * BLK, :] = window(
-            tile + h * BLK, BLK, 2 * tile, pw, row_start + h * BLK, col_start
+        cur[h * BLK : (h + 1) * BLK, :] = window(tile + h * BLK, BLK, 2 * tile, pw) + diagonal(
+            BLK, pw, row_start + h * BLK - col_start
         )
 
     def pair(rows, cols):
         return x_hi[rows, cols], x_lo[rows, cols]
 
     def place(b):
-        return pl.ds(b * BLK if isinstance(b, int) else pl.multiple_of(b * BLK, BLK), BLK)
+        return slice(b * BLK, (b + 1) * BLK)
 
     def solve(rows, b):
         panel = dot3(split(stack[rows, place(b)]), (inv_hi[...], inv_lo[...]))
@@ -158,7 +172,7 @@
 
     def reduce(rows, b):
         stack[rows, place(b)] = stack[rows, place(b)] - dot3(
-            pair(rows, slice(None)), pair(place(b), slice(None))
+            pair(rows, slice(0, b * BLK)), pair(place(b), slice(0, b * BLK))
         )
 
     def downdate(h, b):
@@ -168,46 +182,41 @@
 
     def finish(b):
         inv_hi[...], inv_lo[...] = split(upper[:, BLK:])
-        solve(slice(0, tile), b)
-
-    work[:, BLK:] = (
-        lax.broadcasted_iota(jnp.int32, (BLK, BLK), 0) == lax.broadcasted_iota(jnp.int32, (BLK, BLK), 1)
-    ).astype(F32)
+        solve(slice(b * BLK, tile), b)
+
+    eye = diagonal(BLK, BLK, 0)
+    zeros[...] = jnp.zeros_like(zeros)
+    work[:, BLK:] = eye
     for t in range(lead_chunks):
         embed(t)
     for t in range(lead_chunks):
         lead_window(t)
-    x_hi[...] = jnp.zeros_like(x_hi)
-    x_lo[...] = jnp.zeros_like(x_lo)
 
     outer = range(lead_chunks, chunks)
     fillers = [lambda t=t: embed(t) for t in outer] + [lambda t=t: lead_window(t) for t in outer]
     fillers += [lambda h=h: cur_window(h) for h in range(lead_chunks)]
     work[:, :BLK] = stack[0:BLK, 0:BLK]
-    factor_block(work, upper, fillers)
+    factor_block(work, upper, zeros, fillers)
     finish(0)
 
-    def step(b, carry):
-        work[:, :BLK] = stack[place(b), place(b)] - dot3(
-            pair(place(b), slice(None)), pair(place(b), slice(None))
-        )
-        work[:, BLK:] = (
-            lax.broadcasted_iota(jnp.int32, (BLK, BLK), 0) == lax.broadcasted_iota(jnp.int32, (BLK, BLK), 1)
-        ).astype(F32)
+    def step(b):
+        done = slice(0, b * BLK)
+        work[:, :BLK] = stack[place(b), place(b)] - dot3(pair(place(b), done), pair(place(b), done))
+        work[:, BLK:] = eye
 
         def advance(t):
             rows = slice(t * BLK, (t + 1) * BLK)
             solve(rows, b - 1)
             reduce(rows, b)
 
-        tasks = [lambda t=t: reduce(slice(t * BLK, (t + 1) * BLK), b) for t in range(lead_chunks)]
+        tasks = [lambda t=t: reduce(slice(t * BLK, (t + 1) * BLK), b) for t in range(b, lead_chunks)]
         tasks += [lambda t=t: advance(t) for t in outer]
         tasks += [lambda h=h: downdate(h, b - 1) for h in range(lead_chunks)]
-        factor_block(work, upper, tasks)
+        factor_block(work, upper, zeros, tasks)
         finish(b)
-        return carry
-
-    lax.fori_loop(1, lead_chunks, step, 0)
+
+    for b in range(1, lead_chunks):
+        step(b)
 
     is_lead = row_index == 0
     last = lead_chunks - 1
@@ -399,7 +408,6 @@
         out_specs=vm,
         scratch_shapes=[
             pltpu.VMEM((n, feat), BF16),
-            pltpu.VMEM((n, feat), BF16),
             pltpu.VMEM((n, 1), F32),
             pltpu.VMEM((SUB, n), F32),
             pltpu.VMEM((n, 1), F32),
@@ -412,6 +420,7 @@
             pltpu.VMEM((n, tile), BF16),
             pltpu.VMEM((BLK, BLK), BF16),
             pltpu.VMEM((BLK, BLK), BF16),
+            pltpu.VMEM((SUB, BLK), F32),
         ],
         compiler_params=pltpu.CompilerParams(vmem_limit_bytes=60 * 1024 * 1024),
     )(bins, hidden_weight, hidden_bias.reshape(1, -1), feature_weight)

time: 47.4 us -> 37.6 us (0.79)
  Pallas kernels: 45.7 us -> 36 us
    pallas_call x1, Pallas kernels: 31 us -> 21.3 us  [per_device(): pl.pallas_call(lambda *refs: main_kernel(pw, d_in, *refs), out_shape=jax....]
where the time goes in v2:
time: 37.6 us; the launch traced here: 37.4 us
  Pallas kernels  36 us (96%)
  local copies, waits for them, and re-layouts  0.73 us (2%)
  other arithmetic  0.69 us (2%)
    pallas_call x1, Pallas kernels, per_device(): pl.pallas_call(lambda *refs: main_kernel(pw, d_in, *refs), out_shape=jax....  21.3 us
    pallas_call x1, Pallas kernels, gather_bins(): pl.pallas_call(gather_kernel, out_shape=jax.ShapeDtypeStruct((packed.shap...  14.7 us

profile of v2, /device:TPU:11, one launch (start us, length us, event | category | flops | bytes accessed | tf_op | source)
XLA Modules:
  0.0 37.4 jit_solution(6915599128956131465)
XLA Ops:
  0.0 0.0 copy-start.1
  0.0 0.0 copy-start
  0.0 0.7 %copy-done.1 = s32[64]{0:T(128)S(1)} copy-done((s32[64]{0:T(128)S(1)}, s32[64]{0:T(128)}, u32[]{:S(2)}) %copy-start.1) | copy-done | bytes 280
  0.7 0.1 broadcast_in_dim.2
  0.7 0.0 copy-done
  0.7 0.7 %pad_maximum_fusion.x_ref = bf16[64,128]{1,0:T(8,128)(2,1)} fusion(bf16[64,64]{1,0:T(8,128)(2,1)S(1)} %broadcast_in_dim.2, bf16[64,64]{1,0:T(8,128)(2,1)S(1)} %copy-done), kind=kLoop, calls=%fused_computation | loop fusion | flops 32768 | bytes 32768 | tf_op jit(solution)/shard_map/concatenate | solution.py:400
  1.4 14.7 %shard_map.55.refs_0_ = bf16[2048,128]{1,0:T(8,128)(2,1)} custom-call(bf16[64,128]{1,0:T(8,128)(2,1)} %pad_maximum_fusion.x_ref), custom_call_target="tpu_custom_call" | custom-call | tf_op jit(solution)/shard_map/pallas_call | solution.py:378
  16.1 21.3 %shard_map.56 = f32[512,256]{1,0:T(8,128)} custom-call(bf16[2048,128]{1,0:T(8,128)(2,1)} %shard_map.55.refs_0_, bf16[64,1024]{1,0:T(8,128)(2,1)} %refs_1_.1, f32[1,1024]{1,0:T(1,128)} %bitcast.1, bf16[1024,256]{1,0:T(8,128)(2,1)} %refs_3_.1), custom_call_target="tpu_custom_call" | custom-call | tf_op jit(solution)/shard_map/pallas_call | solution.py:404
  (1 shorter events, 0.0 us)
Async XLA Ops:
  0.0 0.7 %copy-start.1 = (s32[64]{0:T(128)S(1)}, s32[64]{0:T(128)}, u32[]{:S(2)}) copy-start(s32[64]{0:T(128)} %param.6) | copy-start | bytes 772
  0.0 0.7 %copy-start = (bf16[64,64]{1,0:T(8,128)(2,1)S(1)}, bf16[64,64]{1,0:T(8,128)(2,1)}, u32[]{:S(2)}) copy-start(bf16[64,64]{1,0:T(8,128)(2,1)} %param.5) | copy-start | bytes 24580
